TPU v7x, 32 devices: a whole 2x2x4 slice. The times are simulated.
32 devices in a mesh: dp: 8 (over z, y), head: 4 (over x, core).
Axes of the slice: x: 2, y: 2, z: 4, core: 2. Of those that a mesh axis runs over, the one named last changes fastest.
Arguments:
- tokens: bfloat16 [32768, 512], P(('dp', 'head')), may hold values from -6 to 6
- segments: int32 [32768], P('dp'), may hold values from 0 to 255, never falling along the last dimension, each value on 1 to 256 neighbouring positions
- out_grad: bfloat16 [32768, 512], P(('dp', 'head')), may hold values from -6 to 6
- norm_params: float32 [4, 512], replicated, may hold values from -0.6 to 1.3
- norm_first: float32 [4, 512], replicated, may hold values from -0.0024414062 to 0.0024414062
- norm_second: float32 [4, 512], replicated, may hold values from 7.947286e-08 to 1.2715658e-06
- qkv_weight: float32 [512, 1536], P(None, 'head'), may hold values from -0.25 to 0.25
- qkv_moment: float32 [512, 1536], P(None, 'head'), may hold values from -0.0078125 to 0.0078125
- out_weight: float32 [512, 512], P('head'), may hold values from -2 to 2
- out_moment: float32 [512, 512], P('head'), may hold values from -0.0078125 to 0.0078125
- up_weight: float32 [512, 2048], P(None, ('dp', 'head')), may hold values from -0.25 to 0.25
- up_moment: float32 [512, 2048], P(None, ('dp', 'head')), may hold values from -0.0078125 to 0.0078125
- down_weight: float32 [512, 2048], P(None, ('dp', 'head')), may hold values from -0.125 to 0.125
- down_moment: float32 [512, 2048], P(None, ('dp', 'head')), may hold values from -0.0078125 to 0.0078125
Outputs:
- layer_out: bfloat16 [32768, 512], P(('dp', 'head'))
- input_grad: float32 [32768, 512], P(('dp', 'head'))
- grad_norm: float32 [], replicated
- clipped_grads: float32 [4, 512], replicated
- new_norm_first: float32 [4, 512], replicated
- new_norm_second: float32 [4, 512], replicated
- new_qkv_weight: float32 [512, 1536], P(None, 'head')
- new_qkv_moment: float32 [512, 1536], P(None, 'head')
- new_out_weight: float32 [512, 512], P('head')
- new_out_moment: float32 [512, 512], P('head')
- new_up_weight: float32 [512, 2048], P(None, ('dp', 'head'))
- new_up_moment: float32 [512, 2048], P(None, ('dp', 'head'))
- new_down_weight: float32 [512, 2048], P(None, ('dp', 'head'))
- new_down_moment: float32 [512, 2048], P(None, ('dp', 'head'))
Inputs may be any that keep to these rules, and one draw needn't show every extreme that they name: `segments`: segment ids never fall along the rows; each id covers 1 to 256 consecutive rows.
All inputs are finite; a program needn't handle non-finite values.
Results may differ from a plain program's by a relative error of at most 0.028.
Values may be sent and summed in bfloat16 or wider, within the bound.
A program may use at most 128 MiB of HBM per device.

v0:
```python
import math
import jax
import jax.numpy as jnp
from jax import lax
from jax.sharding import PartitionSpec as P

HEAD_DIM = 64
FF = 2048
SEQ = 512
NS_STEPS = 5
neg_fill = -1000000000.0
norm_eps = 1e-05
ns_a = 3.4445
ns_b = -4.775
ns_c = 2.0315
momentum_decay = 0.95
muon_rate = 0.5
muon_decay = 0.01
beta_one = 0.9
beta_two = 0.95


def normalize(values, gain, shift):
    mean = jnp.mean(values, axis=-1, keepdims=True)
    centered = values - mean
    factor = lax.rsqrt(jnp.mean(centered * centered, axis=-1, keepdims=True) + norm_eps)
    plain = centered * factor
    return (plain * gain + shift, plain, factor)


def normalize_back(upper, plain, factor, gain):
    inner = upper * gain
    lower = factor * (
        inner
        - jnp.mean(inner, axis=-1, keepdims=True)
        - plain * jnp.mean(inner * plain, axis=-1, keepdims=True)
    )
    return (lower, jnp.sum(upper * plain, axis=0), jnp.sum(upper, axis=0))


def masked_scores(query, keys, segment):
    scores = jnp.einsum(
        "qhd,khd->hqk", query, keys, preferred_element_type=jnp.float32
    ) * HEAD_DIM ** (-0.5)
    same = segment[:, None] == segment[None, :]
    return jnp.where(same[None], scores, neg_fill)


def attend_forward(block):
    query, keys, values, segment = block
    scores = masked_scores(query, keys, segment)
    top = jnp.max(scores, axis=-1, keepdims=True)
    weights = jnp.exp(scores - top)
    total = jnp.sum(weights, axis=-1, keepdims=True)
    probs = (weights / total).astype(jnp.bfloat16)
    context = jnp.einsum("hqk,khd->qhd", probs, values, preferred_element_type=jnp.float32)
    return (context.astype(jnp.bfloat16), top + jnp.log(total))


def attend_backward(block):
    query, keys, values, segment, context_grad, lse = block
    scores = masked_scores(query, keys, segment)
    probs = jnp.exp(scores - lse)
    probs_low = probs.astype(jnp.bfloat16)
    probs_grad = jnp.einsum(
        "qhd,khd->hqk", context_grad, values, preferred_element_type=jnp.float32
    )
    inner = jnp.sum(probs * probs_grad, axis=-1, keepdims=True)
    score_grad = (probs * (probs_grad - inner)).astype(jnp.bfloat16)
    query_grad = jnp.einsum(
        "hqk,khd->qhd", score_grad, keys, preferred_element_type=jnp.float32
    ) * HEAD_DIM ** (-0.5)
    key_grad = jnp.einsum(
        "hqk,qhd->khd", score_grad, query, preferred_element_type=jnp.float32
    ) * HEAD_DIM ** (-0.5)
    value_grad = jnp.einsum(
        "hqk,qhd->khd", probs_low, context_grad, preferred_element_type=jnp.float32
    )
    return jnp.stack([query_grad, key_grad, value_grad], axis=2).astype(jnp.bfloat16)


def gram_left(block):
    return lax.dot_general(
        block, block, (((1,), (1,)), ((), ())), preferred_element_type=jnp.float32
    )


def gram_right(block):
    return lax.dot_general(
        block, block, (((0,), (0,)), ((), ())), preferred_element_type=jnp.float32
    )


def squares_of(moment, grad, weight):
    return (
        jnp.stack([jnp.sum(moment * moment), jnp.sum(moment * grad), jnp.sum(grad * grad)]) * weight
    )


def shards(
    tokens,
    segments,
    out_grad,
    norm_params,
    norm_first,
    norm_second,
    qkv_weight,
    qkv_moment,
    out_weight,
    out_moment,
    up_weight,
    up_moment,
    down_weight,
    down_moment,
):
    width = tokens.shape[1]
    group = segments.shape[0]
    narrow = out_weight.shape[0]
    heads_here = narrow // HEAD_DIM
    sequences = group // SEQ
    inputs = tokens.astype(jnp.float32)
    first, first_plain, first_factor = normalize(inputs, norm_params[0], norm_params[1])
    first_all = lax.all_gather(first.astype(jnp.bfloat16), "head", axis=0, tiled=True)
    qkv_low = qkv_weight.astype(jnp.bfloat16)
    out_low = out_weight.astype(jnp.bfloat16)
    mixed = jnp.dot(first_all, qkv_low, preferred_element_type=jnp.float32).astype(jnp.bfloat16)
    mixed = mixed.reshape(sequences, SEQ, heads_here, 3, HEAD_DIM)
    segment_rows = segments.reshape(sequences, SEQ)
    query = mixed[:, :, :, 0]
    keys = mixed[:, :, :, 1]
    values = mixed[:, :, :, 2]
    context, lse = lax.map(attend_forward, (query, keys, values, segment_rows))
    context = context.reshape(group, narrow)
    context_rows = lax.all_to_all(context, "head", split_axis=0, concat_axis=1, tiled=True)
    out_full = lax.all_gather(out_low, "head", axis=0, tiled=True)
    attended = jnp.dot(context_rows, out_full, preferred_element_type=jnp.float32)
    middle = inputs + attended
    second, second_plain, second_factor = normalize(middle, norm_params[2], norm_params[3])
    second_low = second.astype(jnp.bfloat16)
    up_all, down_all = (
        lax.all_gather(up_weight.astype(jnp.bfloat16), ("dp", "head"), axis=1, tiled=True),
        lax.all_gather(down_weight.astype(jnp.bfloat16), ("dp", "head"), axis=1, tiled=True),
    )
    hidden = jnp.dot(second_low, up_all, preferred_element_type=jnp.float32)
    switch = jax.nn.sigmoid(1.702 * hidden)
    active = (hidden * switch).astype(jnp.bfloat16)
    result = middle + lax.dot_general(
        active, down_all, (((1,), (1,)), ((), ())), preferred_element_type=jnp.float32
    )
    layer_out = result.astype(jnp.bfloat16)
    down_grad = lax.dot_general(
        out_grad, active, (((0,), (0,)), ((), ())), preferred_element_type=jnp.float32
    )
    active_grad = jnp.dot(out_grad, down_all, preferred_element_type=jnp.float32)
    hidden_grad = (active_grad * (switch + 1.702 * hidden * switch * (1.0 - switch))).astype(
        jnp.bfloat16
    )
    up_grad = lax.dot_general(
        second_low, hidden_grad, (((0,), (0,)), ((), ())), preferred_element_type=jnp.float32
    )
    second_grad = lax.dot_general(
        hidden_grad, up_all, (((1,), (1,)), ((), ())), preferred_element_type=jnp.float32
    )
    up_part, down_part = (
        lax.psum_scatter(up_grad, ("dp", "head"), scatter_dimension=1, tiled=True),
        lax.psum_scatter(down_grad, ("dp", "head"), scatter_dimension=1, tiled=True),
    )
    middle_lower, gain_two, shift_two = normalize_back(
        second_grad, second_plain, second_factor, norm_params[2]
    )
    middle_grad = out_grad.astype(jnp.float32) + middle_lower
    attended_low = middle_grad.astype(jnp.bfloat16)
    rows_grad = lax.dot_general(
        attended_low, out_full, (((1,), (1,)), ((), ())), preferred_element_type=jnp.float32
    ).astype(jnp.bfloat16)
    context_grad = lax.all_to_all(rows_grad, "head", split_axis=1, concat_axis=0, tiled=True)
    whole_out = lax.dot_general(
        context_rows, attended_low, (((0,), (0,)), ((), ())), preferred_element_type=jnp.float32
    )
    out_part = lax.psum_scatter(
        whole_out.astype(jnp.bfloat16), "head", scatter_dimension=0, tiled=True
    )
    context_grad = context_grad.reshape(sequences, SEQ, heads_here, HEAD_DIM)
    mixed_grad = lax.map(attend_backward, (query, keys, values, segment_rows, context_grad, lse))
    mixed_grad = mixed_grad.reshape(group, 3 * narrow)
    qkv_part = lax.dot_general(
        first_all, mixed_grad, (((0,), (0,)), ((), ())), preferred_element_type=jnp.float32
    )
    mixed_rows = lax.all_to_all(mixed_grad, "head", split_axis=0, concat_axis=1, tiled=True)
    qkv_full = lax.all_gather(qkv_low, "head", axis=1, tiled=True)
    first_grad = lax.dot_general(
        mixed_rows, qkv_full, (((1,), (1,)), ((), ())), preferred_element_type=jnp.float32
    )
    input_lower, gain_one, shift_one = normalize_back(
        first_grad, first_plain, first_factor, norm_params[0]
    )
    input_grad = middle_grad + input_lower
    qkv_sum, out_sum = (
        lax.psum(qkv_part.astype(jnp.bfloat16), "dp").astype(jnp.float32),
        lax.psum(out_part, "dp").astype(jnp.float32),
    )
    leading = (lax.axis_index("dp") == 0).astype(jnp.float32)
    moments = [qkv_moment, out_moment, up_moment, down_moment]
    grads = [qkv_sum, out_sum, up_part, down_part]
    stats = jnp.stack(
        [
            squares_of(qkv_moment, qkv_sum, leading),
            squares_of(out_moment, out_sum, leading),
            squares_of(up_moment, up_part, 1.0),
            squares_of(down_moment, down_part, 1.0),
        ]
    )
    vector_part = jnp.stack([gain_one, shift_one, gain_two, shift_two])
    vector_sum, stat_sum = lax.psum((vector_part, stats), ("dp", "head"))
    grad_norm = jnp.sqrt(jnp.sum(stat_sum[:, 2]) + jnp.sum(vector_sum * vector_sum))
    clip = jnp.minimum(1.0, 1.0 / (grad_norm + 1e-06))
    sizes = jnp.sqrt(
        momentum_decay * momentum_decay * stat_sum[:, 0]
        + 2.0 * momentum_decay * clip * stat_sum[:, 1]
        + clip * clip * stat_sum[:, 2]
    )
    new_moments = [momentum_decay * moments[index] + clip * grads[index] for index in range(4)]
    starts = [
        (new_moments[index] / (sizes[index] + 1e-07)).astype(jnp.bfloat16) for index in range(4)
    ]
    up_block, down_block = (
        lax.all_gather(starts[2], "dp", axis=1, tiled=True),
        lax.all_gather(starts[3], "dp", axis=1, tiled=True),
    )
    blocks = [starts[0], starts[1], up_block, down_block]
    for turn in range(NS_STEPS):
        partials = (
            gram_left(blocks[0]),
            gram_right(blocks[1]),
            gram_left(blocks[2]),
            gram_left(blocks[3]),
        )
        grams = (
            lax.psum(partials[0].astype(jnp.bfloat16), "head").astype(jnp.float32),
            lax.psum(partials[1].astype(jnp.bfloat16), "head").astype(jnp.float32),
            lax.psum(partials[2].astype(jnp.bfloat16), "head").astype(jnp.float32),
            lax.psum(partials[3].astype(jnp.bfloat16), "head").astype(jnp.float32),
        )
        updated = []
        for index in range(4):
            gram = grams[index].astype(jnp.bfloat16)
            mix = (
                ns_b * gram.astype(jnp.float32)
                + ns_c * jnp.dot(gram, gram, preferred_element_type=jnp.float32)
            ).astype(jnp.bfloat16)
            if index == 1:
                product = jnp.dot(blocks[index], mix, preferred_element_type=jnp.float32)
            else:
                product = jnp.dot(mix, blocks[index], preferred_element_type=jnp.float32)
            updated.append(
                (ns_a * blocks[index].astype(jnp.float32) + product).astype(jnp.bfloat16)
            )
        blocks = updated
    share = up_weight.shape[1]
    offset = lax.axis_index("dp") * share
    owned = [
        blocks[0],
        blocks[1],
        lax.dynamic_slice_in_dim(blocks[2], offset, share, 1),
        lax.dynamic_slice_in_dim(blocks[3], offset, share, 1),
    ]
    weights = [qkv_weight, out_weight, up_weight, down_weight]
    factors = [
        math.sqrt(3.0),
        math.sqrt(SEQ / 8.0),
        math.sqrt(max(1.0, FF / width)),
        math.sqrt(max(1.0, FF / width)),
    ]
    new_weights = [
        weights[index] * (1.0 - muon_rate * muon_decay)
        - muon_rate * factors[index] * owned[index].astype(jnp.float32)
        for index in range(4)
    ]
    clipped = clip * vector_sum
    first_new = beta_one * norm_first + (1.0 - beta_one) * clipped
    second_new = beta_two * norm_second + (1.0 - beta_two) * clipped * clipped
    return (
        layer_out,
        input_grad,
        grad_norm,
        clipped,
        first_new,
        second_new,
        new_weights[0],
        new_moments[0],
        new_weights[1],
        new_moments[1],
        new_weights[2],
        new_moments[2],
        new_weights[3],
        new_moments[3],
    )


def solution(mesh):
    placed = (
        P(("dp", "head"), None),
        P("dp"),
        P(("dp", "head"), None),
        P(),
        P(),
        P(),
        P(None, "head"),
        P(None, "head"),
        P("head", None),
        P("head", None),
        P(None, ("dp", "head")),
        P(None, ("dp", "head")),
        P(None, ("dp", "head")),
        P(None, ("dp", "head")),
    )
    return jax.shard_map(
        shards,
        mesh=mesh,
        in_specs=placed,
        out_specs=(
            P(("dp", "head"), None),
            P(("dp", "head"), None),
            P(),
            P(),
            P(),
            P(),
            P(None, "head"),
            P(None, "head"),
            P("head", None),
            P("head", None),
            P(None, ("dp", "head")),
            P(None, ("dp", "head")),
            P(None, ("dp", "head")),
            P(None, ("dp", "head")),
        ),
        check_vma=False,
    )
```

profile of v0, /device:TPU:0, one launch (start us, length us, event | category | flops | bytes accessed | tf_op | source)
XLA Modules:
  0.0 1169.6 jit_solution(14758495943311568836)
XLA Ops:
  13.5 35.1 %all-gather.5.cloned.1.call-done = bf16[4096,512]{0,1:T(8,128)(2,1)} async-done(((bf16[1024,512]{0,1:T(8,128)(2,1)}), bf16[4096,512]{0,1:T(8,128)(2,1)}) %all-gather.5.cloned.1.call-update) | async-done | bytes 4194320 | tf_op jit(solution)/shard_map/all_gather | solution.py:123
  48.6 6.2 convolution_convert_fusion.2
  54.8 4.8 copy.76
  59.6 3.3 copy.103
  65.1 40.1 %while.22 = (s32[]{:T(128)}, bf16[8,512,2,64]{1,3,2,0:T(8,128)(2,1)}, f32[8,2,512,1]{2,1,3,0:T(2,128)}, bf16[8,512,2,64]{1,3,2,0:T(8,128)(2,1)}, s32[8,512]{1,0:...) while((s32[]{:T(128)}, ...), condition=%wide.region_5.6_spmd, body=%wide.region_2.5_spmd.sunk | while | flops 140835840 | bytes 7905881 | solution.py:132
  105.2 3.5 copy.80
  108.7 2.5 all_to_all.40
  111.2 2.6 copy.81
  113.8 3.6 all-to-all-start
  118.9 17.6 %all_gather.22 = bf16[512,512]{1,0:T(8,128)(2,1)} all-gather(bf16[128,512]{1,0:T(8,128)(2,1)S(1)} %convert_element_type.448), channel_id=1, replica_groups=mesh['dp'=8,'head'=4] {'head'}, dimensions={0}, use_global_device_ids=true | all-gather | bytes 655360 | tf_op jit(solution)/shard_map/all_gather | solution.py:135
  140.3 8.4 multiply_convert_fusion.2
  148.7 18.5 %all-gather.9.cloned.1.call-done = bf16[512,2048]{0,1:T(8,128)(2,1)} async-done(((bf16[512,64]{0,1:T(8,128)(2,1)}), bf16[512,2048]{0,1:T(8,128)(2,1)}) %all-gather.9.cloned.1.call-update) | async-done | bytes 2097168 | tf_op jit(solution)/shard_map/all_gather | solution.py:142
  167.2 8.4 multiply_convert_fusion.1
  175.7 4.2 fusion.268
  179.9 2.9 copy.84
  182.8 3.0 multiply_reduce_fusion.1
  190.0 4.2 all-to-all-start.1
  194.3 2.8 convolution_convert_fusion.24
  197.5 11.2 all-to-all-done.1
  208.7 3.0 copy.85
  216.4 81.9 %while.23 = (s32[]{:T(128)}, bf16[8,512,2,3,64]{1,4,2,3,0:T(8,128)(2,1)}, bf16[8,512,2,64]{1,3,2,0:T(8,128)(2,1)}, s32[8,512]{1,0:T(8,128)}, bf16[8,512,2,64]{1,...) while((s32[]{:T(128)}, ...), condition=%wide.region_12.13_spmd, body=%wide.region_10.12_spmd.sunk | while | flops 342031360 | bytes 18380900 | solution.py:184
  298.4 3.7 copy.90
  305.4 3.1 convolution_convert_fusion.25
  309.2 7.3 fusion.263
  316.7 6.9 convolution_bitcast_fusion
  323.6 6.0 all_to_all.47
  329.7 4.6 copy.91
  334.2 4.8 all-to-all-start.2
  339.1 41.0 %all-reduce.14.cloned.1.call-done = (bf16[128,512]{1,0:T(8,128)(2,1)}, bf16[512,384]{1,0:T(8,128)(2,1)}) async-done(((bf16[128,512]{1,0:T(8,128)(2,1)}, bf16[512,384]{1,0:T(8,128)(2,1)}), (bf16[128,512]{1,0:T(8,128)(2,1)}, bf16[512,384]{1,0:T(8,128)(2,1)})) %all-reduce.14.cloned.1.call-update) | async-done | bytes 524304 | tf_op jit(solution)/shard_map/psum | solution.py:200
  382.2 2.5 maximum_multiply_fusion
  386.3 2.5 maximum_multiply_fusion.1
  388.8 12.2 %all-gather.11.cloned.1.call-done = bf16[512,1536]{1,0:T(8,128)(2,1)} async-done(((bf16[512,384]{1,0:T(8,128)(2,1)}), bf16[512,1536]{1,0:T(8,128)(2,1)}) %all-gather.11.cloned.1.call-update) | async-done | bytes 1572880 | tf_op jit(solution)/shard_map/all_gather | solution.py:190
  401.0 6.1 fusion.269
  407.1 2.9 copy.92
  410.0 3.0 fusion.54
  413.6 130.7 %reduce-scatter.6.cloned.1.call-done = f32[512,64]{0,1:T(8,128)} async-done(((f32[512,2048]{0,1:T(8,128)}), f32[512,64]{0,1:T(8,128)}) %reduce-scatter.6.cloned.1.call-update) | async-done | bytes 131088 | tf_op jit(solution)/shard_map/reduce_scatter | solution.py:165
  545.9 137.6 %reduce-scatter.8.cloned.1.call-done = f32[512,64]{0,1:T(8,128)} async-done(((f32[512,2048]{0,1:T(8,128)}), f32[512,64]{0,1:T(8,128)}) %reduce-scatter.8.cloned.1.call-update) | async-done | bytes 131088 | tf_op jit(solution)/shard_map/reduce_scatter | solution.py:166
  685.2 4.0 maximum_bitcast_fusion
  690.4 37.2 %all-reduce = (f32[4,3]{1,0:T(4,128)S(1)}, f32[4,512]{1,0:T(4,128)}) all-reduce(f32[4,3]{1,0:T(4,128)} %pad_maximum_fusion.1, f32[4,512]{1,0:T(4,128)} %pad_maximum_fusion), channel_id=1, replica_groups=mesh['dp'=8,'head'=4] {'dp','head'}, use_global_device_ids=true, to_apply=%region_32.33 | all-reduce | flops 2060 | bytes 16480 | tf_op jit(solution)/shard_map/psum | solution.py:214
  737.7 31.5 %all_gather.27 = bf16[512,512]{0,1:T(8,128)(2,1)S(1)} all-gather(bf16[512,64]{0,1:T(8,128)(2,1)S(1)} %get-tuple-element.241), channel_id=1, replica_groups=mesh['dp'=8,'head'=4] {'dp'}, dimensions={1}, use_global_device_ids=true | all-gather | bytes 589824 | tf_op jit(solution)/shard_map/all_gather | solution.py:228
  772.0 31.2 %all_gather.26 = bf16[512,512]{0,1:T(8,128)(2,1)S(1)} all-gather(bf16[512,64]{0,1:T(8,128)(2,1)S(1)} %get-tuple-element.243), channel_id=1, replica_groups=mesh['dp'=8,'head'=4] {'dp'}, dimensions={1}, use_global_device_ids=true | all-gather | bytes 589824 | tf_op jit(solution)/shard_map/all_gather | solution.py:227
  808.4 51.9 %all-reduce.24.cloned.1.call-done = (bf16[512,512]{1,0:T(8,128)(2,1)}, bf16[512,512]{1,0:T(8,128)(2,1)}, bf16[512,512]{1,0:T(8,128)(2,1)}, bf16[512,512]{1,0:T(8,128)(2,1)}) async-done(((bf16[512,512]{1,0:T(8,128)(2,1)}, bf16[512,512]{1,0:T(8,128)(2,1)}, bf16[512,512]{1,0:T(8,128)(2,1)}, bf16[512,512]{1,0:T(8,128)(2,1)}), (bf16[512,512]{1,0:T(8,128)(2,1)}, bf16[512,512]{1,0:T(8,128)(2,1)}, ...) | async-done | bytes 2097168 | tf_op jit(solution)/shard_map/psum | solution.py:239
  860.3 3.5 fusion.100
  866.2 3.5 fusion.96
  875.4 2.8 fusion.104
  879.5 52.1 %all-reduce.22.cloned.1.call-done = (bf16[512,512]{1,0:T(8,128)(2,1)}, bf16[512,512]{1,0:T(8,128)(2,1)}, bf16[512,512]{1,0:T(8,128)(2,1)}, bf16[512,512]{1,0:T(8,128)(2,1)}) async-done(((bf16[512,512]{1,0:T(8,128)(2,1)}, bf16[512,512]{1,0:T(8,128)(2,1)}, bf16[512,512]{1,0:T(8,128)(2,1)}, bf16[512,512]{1,0:T(8,128)(2,1)}), (bf16[512,512]{1,0:T(8,128)(2,1)}, bf16[512,512]{1,0:T(8,128)(2,1)}, ...) | async-done | bytes 2097168 | tf_op jit(solution)/shard_map/psum | solution.py:239
  931.6 3.5 fusion.101
  937.6 3.5 fusion.97
  943.6 2.8 fusion.130
  948.4 3.0 fusion.105
  953.8 52.1 %all-reduce.20.cloned.1.call-done = (bf16[512,512]{1,0:T(8,128)(2,1)}, bf16[512,512]{1,0:T(8,128)(2,1)}, bf16[512,512]{1,0:T(8,128)(2,1)}, bf16[512,512]{1,0:T(8,128)(2,1)}) async-done(((bf16[512,512]{1,0:T(8,128)(2,1)}, bf16[512,512]{1,0:T(8,128)(2,1)}, bf16[512,512]{1,0:T(8,128)(2,1)}, bf16[512,512]{1,0:T(8,128)(2,1)}), (bf16[512,512]{1,0:T(8,128)(2,1)}, bf16[512,512]{1,0:T(8,128)(2,1)}, ...) | async-done | bytes 2097168 | tf_op jit(solution)/shard_map/psum | solution.py:239
  1006.0 3.4 fusion.102
  1011.8 3.5 fusion.98
  1021.0 2.5 fusion.106
  1025.1 6.8 add_convert_fusion
  1034.8 42.2 %all-reduce.18.cloned.1.call-done = (bf16[512,512]{1,0:T(8,128)(2,1)}, bf16[512,512]{1,0:T(8,128)(2,1)}, bf16[512,512]{1,0:T(8,128)(2,1)}, bf16[512,512]{1,0:T(8,128)(2,1)}) async-done(((bf16[512,512]{1,0:T(8,128)(2,1)}, bf16[512,512]{1,0:T(8,128)(2,1)}, bf16[512,512]{1,0:T(8,128)(2,1)}, bf16[512,512]{1,0:T(8,128)(2,1)}), (bf16[512,512]{1,0:T(8,128)(2,1)}, bf16[512,512]{1,0:T(8,128)(2,1)}, ...) | async-done | bytes 2097168 | tf_op jit(solution)/shard_map/psum | solution.py:239
  1077.0 3.5 fusion.103
  1083.0 3.4 fusion.99
  1092.1 2.6 fusion.107
  1096.0 3.6 fusion.53
  1099.6 2.9 copy.97
  1103.8 44.4 %all-reduce.16.cloned.1.call-done = (bf16[512,512]{1,0:T(8,128)(2,1)}, bf16[512,512]{1,0:T(8,128)(2,1)}, bf16[512,512]{1,0:T(8,128)(2,1)}, bf16[512,512]{1,0:T(8,128)(2,1)}) async-done(((bf16[512,512]{1,0:T(8,128)(2,1)}, bf16[512,512]{1,0:T(8,128)(2,1)}, bf16[512,512]{1,0:T(8,128)(2,1)}, bf16[512,512]{1,0:T(8,128)(2,1)}), (bf16[512,512]{1,0:T(8,128)(2,1)}, bf16[512,512]{1,0:T(8,128)(2,1)}, ...) | async-done | bytes 2097168 | tf_op jit(solution)/shard_map/psum | solution.py:239
  1148.2 3.2 fusion.112
  1157.0 2.8 fusion.127
  (338 shorter events, 220.8 us)
Async XLA Ops:
  7.2 2.1 copy-start.41
  7.2 41.4 %all-gather.5.cloned.1.call-start = ((), (), s32[]{:S(2)}) async-start(), calls=%async_computation.6 | async-start | bytes 5242880 | tf_op jit(solution)/shard_map/all_gather | solution.py:123
  8.9 2.4 copy-start.28
  8.9 3.1 copy-start.26
  9.3 3.5 copy-start.13
  9.9 3.0 copy-start.38
  11.3 128.7 %all-gather.7.cloned.1.call-start = ((), (), s32[]{:S(2)}) async-start(), calls=%async_computation.7 | async-start | bytes 2162688 | tf_op jit(solution)/shard_map/all_gather | solution.py:141
  12.0 155.2 %all-gather.9.cloned.1.call-start = ((), (), s32[]{:S(2)}) async-start(), calls=%async_computation.8 | async-start | bytes 2162688 | tf_op jit(solution)/shard_map/all_gather | solution.py:142
  12.8 42.0 %copy-start.10 = (bf16[512,384]{1,0:T(8,128)(2,1)}, bf16[512,384]{1,0:T(8,128)(2,1)S(1)}, u32[]{:S(2)}) copy-start(bf16[512,384]{1,0:T(8,128)(2,1)S(1)} %convert_element_type.446) | copy-start | bytes 1179652
  105.2 6.1 copy-start.4
  105.2 6.1 copy-start.5
  111.2 6.2 copy-start.30
  113.8 3.7 copy-start.11
  113.8 22.7 %all-to-all-start = ((bf16[4,1024,128]{1,2,0:T(8,128)(2,1)}), bf16[4,1024,128]{1,2,0:T(8,128)(2,1)S(1)}, u32[]{:S(2)}, u32[]{:S(2)}) async-start(bf16[4,1024,128]{1,2,0:T(8,128)(2,1)} %copy.81), calls=%async_computation | async-start | bytes 2097152 | tf_op jit(solution)/shard_map/all_to_all | solution.py:134
  139.6 43.2 %copy-start = (f32[1024,512]{0,1:T(8,128)}, f32[1024,512]{0,1:T(8,128)S(1)}, u32[]{:S(2)}) copy-start(f32[1024,512]{0,1:T(8,128)S(1)} %get-tuple-element.263) | copy-start | bytes 6291460
  167.2 8.4 copy-start.49
  175.7 4.2 copy-start.51
  182.8 3.0 copy-start.2
  182.8 3.0 copy-start.7
  185.9 2.4 copy-start.6
  190.0 18.8 %all-to-all-start.1 = ((bf16[1024,4,128]{0,2,1:T(8,128)(2,1)}), bf16[1024,4,128]{0,2,1:T(8,128)(2,1)}, u32[]{:S(2)}, u32[]{:S(2)}) async-start(bf16[1024,4,128]{0,2,1:T(8,128)(2,1)} %bitcast.284), calls=%async_computation.1 | async-start | bytes 2097152 | tf_op jit(solution)/shard_map/all_to_all | solution.py:176
  194.2 114.3 %reduce-scatter.4.cloned.1.call-start = ((), (), s32[]{:S(2)}) async-start(), calls=%async_computation.10 | async-start | bytes 655360 | tf_op jit(solution)/shard_map/reduce_scatter | solution.py:180
  197.1 183.1 %all-reduce.14.cloned.1.call-start = ((), (), s32[]{:S(2)}) async-start(), calls=%async_computation.13 | async-start | bytes 1048576 | tf_op jit(solution)/shard_map/psum | solution.py:200
  302.1 2.1 copy-start.1
  302.1 3.3 copy-start.48
  308.6 92.4 %all-gather.11.cloned.1.call-start = ((), (), s32[]{:S(2)}) async-start(), calls=%async_computation.9 | async-start | bytes 1966080 | tf_op jit(solution)/shard_map/all_gather | solution.py:190
  309.1 235.2 %reduce-scatter.6.cloned.1.call-start = ((), (), s32[]{:S(2)}) async-start(), calls=%async_computation.11 | async-start | bytes 4325376 | tf_op jit(solution)/shard_map/reduce_scatter | solution.py:165
  316.5 367.0 %reduce-scatter.8.cloned.1.call-start = ((), (), s32[]{:S(2)}) async-start(), calls=%async_computation.12 | async-start | bytes 4325376 | tf_op jit(solution)/shard_map/reduce_scatter | solution.py:166
  334.2 50.5 %copy-start.12 = (f32[128,512]{1,0:T(8,128)S(1)}, f32[128,512]{1,0:T(8,128)}, u32[]{:S(2)}) copy-start(f32[128,512]{1,0:T(8,128)} %param.27) | copy-start | bytes 786436
  334.2 66.8 %all-to-all-start.2 = ((bf16[4,1024,384]{1,2,0:T(8,128)(2,1)}), bf16[4,1024,384]{1,2,0:T(8,128)(2,1)}, u32[]{:S(2)}, u32[]{:S(2)}) async-start(bf16[4,1024,384]{1,2,0:T(8,128)(2,1)} %copy.91), calls=%async_computation.2 | async-start | bytes 6291456 | tf_op jit(solution)/shard_map/all_to_all | solution.py:189
  339.1 521.2 %all-reduce.24.cloned.1.call-start = ((), (), s32[]{:S(2)}) async-start(), calls=%async_computation.18 | async-start | bytes 4194304 | tf_op jit(solution)/shard_map/psum | solution.py:239
  410.0 3.0 copy-start.39
  410.0 3.0 copy-start.46
  410.0 3.0 copy-start.47
  410.0 322.7 %copy-start.8 = (bf16[512,384]{1,0:T(8,128)(2,1)S(1)}, bf16[512,384]{1,0:T(8,128)(2,1)}, u32[]{:S(2)}) copy-start(bf16[512,384]{1,0:T(8,128)(2,1)} %get-tuple-element.220) | copy-start | bytes 1179652
  734.8 36.5 %copy-start.22 = (f32[512,64]{0,1:T(8,128)S(1)}, f32[512,64]{0,1:T(8,128)}, u32[]{:S(2)}) copy-start(f32[512,64]{0,1:T(8,128)} %param.29) | copy-start | bytes 393220
  734.8 36.5 %copy-start.23 = (f32[512,64]{0,1:T(8,128)S(1)}, f32[512,64]{0,1:T(8,128)}, u32[]{:S(2)}) copy-start(f32[512,64]{0,1:T(8,128)} %reduce-scatter.6.cloned.1.call-done) | copy-start | bytes 393220
  769.3 35.2 %copy-start.24 = (bf16[512,512]{0,1:T(8,128)(2,1)}, bf16[512,512]{0,1:T(8,128)(2,1)S(1)}, u32[]{:S(2)}) copy-start(bf16[512,512]{0,1:T(8,128)(2,1)S(1)} %all_gather.27) | copy-start | bytes 1572868
  769.3 36.5 %copy-start.32 = (f32[128,512]{1,0:T(8,128)S(1)}, f32[128,512]{1,0:T(8,128)}, u32[]{:S(2)}) copy-start(f32[128,512]{1,0:T(8,128)} %fusion.219) | copy-start | bytes 786436
  770.5 36.3 %copy-start.15 = (f32[512,384]{1,0:T(8,128)S(1)}, f32[512,384]{1,0:T(8,128)}, u32[]{:S(2)}) copy-start(f32[512,384]{1,0:T(8,128)} %fusion.174) | copy-start | bytes 2359300
  803.2 1.3 copy-start.25
  808.2 123.5 %all-reduce.22.cloned.1.call-start = ((), (), s32[]{:S(2)}) async-start(), calls=%async_computation.17 | async-start | bytes 4194304 | tf_op jit(solution)/shard_map/psum | solution.py:239
  866.2 6.0 copy-start.33
  879.5 126.5 %all-reduce.20.cloned.1.call-start = ((), (), s32[]{:S(2)}) async-start(), calls=%async_computation.16 | async-start | bytes 4194304 | tf_op jit(solution)/shard_map/psum | solution.py:239
  953.8 123.2 %all-reduce.18.cloned.1.call-start = ((), (), s32[]{:S(2)}) async-start(), calls=%async_computation.15 | async-start | bytes 4194304 | tf_op jit(solution)/shard_map/psum | solution.py:239
  1011.8 6.0 copy-start.21
  1019.9 1.1 copy-start.18
  1023.5 8.4 copy-start.9
  1024.8 123.3 %all-reduce.16.cloned.1.call-start = ((), (), s32[]{:S(2)}) async-start(), calls=%async_computation.14 | async-start | bytes 4194304 | tf_op jit(solution)/shard_map/psum | solution.py:239
  1032.0 2.3 copy-start.37
  1083.0 5.9 copy-start.19
  1094.7 1.3 copy-start.36
  1099.6 3.0 copy-start.35
  1099.6 3.0 copy-start.44
  1099.6 3.6 copy-start.40
  1099.6 48.6 %copy-start.42 = (bf16[512,512]{0,1:T(8,128)(2,1)S(1)}, bf16[512,512]{0,1:T(8,128)(2,1)}, u32[]{:S(2)}) copy-start(bf16[512,512]{0,1:T(8,128)(2,1)} %fusion.103) | copy-start | bytes 1572868
  1102.6 48.8 %copy-start.43 = (bf16[512,512]{0,1:T(8,128)(2,1)S(1)}, bf16[512,512]{0,1:T(8,128)(2,1)}, u32[]{:S(2)}) copy-start(bf16[512,512]{0,1:T(8,128)(2,1)} %fusion.99) | copy-start | bytes 1572868
  1103.2 50.5 %copy-start.34 = (f32[4,512]{1,0:T(4,128)}, f32[4,512]{1,0:T(4,128)S(1)}, u32[]{:S(2)}) copy-start(f32[4,512]{1,0:T(4,128)S(1)} %get-tuple-element.246) | copy-start | bytes 24580
  1151.4 2.3 copy-start.27
  1151.4 4.0 copy-start.29
  1151.4 5.6 copy-start.17
  1151.4 5.6 copy-start.31
  1153.7 6.1 copy-start.14
  1155.4 4.4 copy-start.50
  (4 other events, 3.9 us)
Sparse Core Ops, SparseCore 0:
  11.4 37.1 all-gather.4
  52.0 56.3 all-gather.6
  111.9 55.3 all-gather.8
  197.8 21.8 reduce-scatter.3
  308.7 71.3 all-reduce.13
  382.1 18.8 all-gather.10
  403.3 140.9 reduce-scatter.5
  546.6 136.9 reduce-scatter.7
  808.3 51.9 all-reduce.23
  879.6 51.9 all-reduce.21
  953.9 52.0 all-reduce.19
  1025.0 51.9 all-reduce.17
  1096.1 52.0 all-reduce.15
where the time goes:
time: 1180 us; the launch traced here: 1170 us
  waiting for transfers between devices  630 us (53%)
  matrix products  239 us (20%)
  blocking collectives  118 us (10%)
  local copies, waits for them, and re-layouts  78.6 us (7%)
  other arithmetic  69.6 us (6%)
  between operations  20.1 us (2%)
  starting transfers between devices  14.3 us (1%)
    psum x5, waiting for transfers between devices, shards(): lax.psum(partials[0].astype(jnp.bfloat16), 'head').astype(jnp.float32)  243 us
    reduce_scatter x1, waiting for transfers between devices, shards(): lax.psum_scatter(down_grad, ('dp', 'head'), scatter_dimension=1, tiled=True)  138 us
    reduce_scatter x1, waiting for transfers between devices, shards(): lax.psum_scatter(up_grad, ('dp', 'head'), scatter_dimension=1, tiled=True)  131 us
    dot_general x15, matrix products, shards(): product = jnp.dot(mix, blocks[index], preferred_element_type=jnp.float32)  45.7 us
    psum x1, waiting for transfers between devices, shards(): lax.psum(out_part, 'dp').astype(jnp.float32)  41 us
    psum x1, blocking collectives, shards(): vector_sum, stat_sum = lax.psum((vector_part, stats), ('dp', 'head'))  37.2 us
    all_gather x1, waiting for transfers between devices, shards(): lax.all_gather(first.astype(jnp.bfloat16), 'head', axis=0, tiled=True)  35.1 us
    all_gather x1, blocking collectives, shards(): lax.all_gather(starts[3], 'dp', axis=1, tiled=True)  31.5 us
  transfers between devices with their start and end apart: 16, of which 12 were waited for; matrix products, arithmetic and copies ran while one was open for 20% of the time, Pallas kernels for 0%

commit v1 on v0

--- a/solution.py
+++ b/solution.py
@@ -211,7 +211,7 @@
         ]
     )
     vector_part = jnp.stack([gain_one, shift_one, gain_two, shift_two])
-    vector_sum, stat_sum = lax.psum((vector_part, stats), ("dp", "head"))
+    vector_sum, stat_sum = lax.psum(lax.psum((vector_part, stats), "head"), "dp")
     grad_norm = jnp.sqrt(jnp.sum(stat_sum[:, 2]) + jnp.sum(vector_sum * vector_sum))
     clip = jnp.minimum(1.0, 1.0 / (grad_norm + 1e-06))
     sizes = jnp.sqrt(

time: 1180 us -> 1190 us (level)
    psum x1 -> x2, blocking collectives: 37.2 us -> 44.7 us  [the longest x1 33.4 us: shards(): lax.psum(lax.psum((vector_part, stats), 'head'), 'dp')]
where the time goes in v1:
time: 1190 us; the launch traced here: 1170 us
  waiting for transfers between devices  625 us (53%)
  matrix products  246 us (21%)
  blocking collectives  124 us (10%)
  local copies, waits for them, and re-layouts  72.8 us (6%)
  other arithmetic  69.1 us (6%)
  between operations  20.2 us (2%)
  starting transfers between devices  14.3 us (1%)
    psum x5, waiting for transfers between devices, shards(): lax.psum(partials[0].astype(jnp.bfloat16), 'head').astype(jnp.float32)  239 us
    reduce_scatter x1, waiting for transfers between devices, shards(): lax.psum_scatter(down_grad, ('dp', 'head'), scatter_dimension=1, tiled=True)  138 us
    reduce_scatter x1, waiting for transfers between devices, shards(): lax.psum_scatter(up_grad, ('dp', 'head'), scatter_dimension=1, tiled=True)  131 us
    dot_general x15, matrix products, shards(): product = jnp.dot(mix, blocks[index], preferred_element_type=jnp.float32)  45.7 us
    psum x1, waiting for transfers between devices, shards(): lax.psum(out_part, 'dp').astype(jnp.float32)  41 us
    all_gather x1, waiting for transfers between devices, shards(): lax.all_gather(first.astype(jnp.bfloat16), 'head', axis=0, tiled=True)  35.7 us
    psum x1, blocking collectives, shards(): lax.psum(lax.psum((vector_part, stats), 'head'), 'dp')  33.4 us
    all_gather x1, blocking collectives, shards(): lax.all_gather(starts[3], 'dp', axis=1, tiled=True)  31.5 us
  transfers between devices with their start and end apart: 16, of which 12 were waited for; matrix products, arithmetic and copies ran while one was open for 20% of the time, Pallas kernels for 0%

profile of v1, /device:TPU:0, one launch (start us, length us, event | category | flops | bytes accessed | tf_op | source)
XLA Modules:
  0.0 1173.1 jit_solution(11436717354638160790)
XLA Ops:
  12.9 35.7 %all-gather.5.cloned.1.call-done = bf16[4096,512]{0,1:T(8,128)(2,1)} async-done(((bf16[1024,512]{0,1:T(8,128)(2,1)}), bf16[4096,512]{0,1:T(8,128)(2,1)}) %all-gather.5.cloned.1.call-update) | async-done | bytes 4194320 | tf_op jit(solution)/shard_map/all_gather | solution.py:123
  48.6 6.2 convolution_convert_fusion.2
  54.8 4.8 copy.76
  59.6 3.3 copy.103
  66.1 41.6 %while.22 = (s32[]{:T(128)}, bf16[8,512,2,64]{1,3,2,0:T(8,128)(2,1)}, f32[8,2,512,1]{2,1,3,0:T(2,128)}, bf16[8,512,2,64]{1,3,2,0:T(8,128)(2,1)}, s32[8,512]{1,0:...) while((s32[]{:T(128)}, ...), condition=%wide.region_5.6_spmd, body=%wide.region_2.5_spmd.sunk | while | flops 140835840 | bytes 7905881 | solution.py:132
  107.7 3.2 copy.80
  113.4 2.6 copy.81
  115.9 3.7 all-to-all-start
  121.0 17.2 %all_gather.22 = bf16[512,512]{1,0:T(8,128)(2,1)} all-gather(bf16[128,512]{1,0:T(8,128)(2,1)S(1)} %convert_element_type.448), channel_id=1, replica_groups=mesh['dp'=8,'head'=4] {'head'}, dimensions={0}, use_global_device_ids=true | all-gather | bytes 655360 | tf_op jit(solution)/shard_map/all_gather | solution.py:135
  142.0 8.4 multiply_convert_fusion.2
  150.5 16.7 %all-gather.9.cloned.1.call-done = bf16[512,2048]{0,1:T(8,128)(2,1)} async-done(((bf16[512,64]{0,1:T(8,128)(2,1)}), bf16[512,2048]{0,1:T(8,128)(2,1)}) %all-gather.9.cloned.1.call-update) | async-done | bytes 2097168 | tf_op jit(solution)/shard_map/all_gather | solution.py:142
  167.2 8.4 multiply_convert_fusion.1
  175.6 4.2 fusion.268
  179.8 2.9 copy.84
  182.7 3.0 multiply_reduce_fusion.1
  189.9 4.2 all-to-all-start.1
  194.2 2.8 convolution_convert_fusion.24
  197.4 11.2 all-to-all-done.1
  208.7 3.0 copy.85
  216.4 81.9 %while.23 = (s32[]{:T(128)}, bf16[8,512,2,3,64]{1,4,2,3,0:T(8,128)(2,1)}, bf16[8,512,2,64]{1,3,2,0:T(8,128)(2,1)}, s32[8,512]{1,0:T(8,128)}, bf16[8,512,2,64]{1,...) while((s32[]{:T(128)}, ...), condition=%wide.region_12.13_spmd, body=%wide.region_10.12_spmd.sunk | while | flops 342031360 | bytes 18380900 | solution.py:184
  298.3 3.7 copy.90
  305.3 3.1 convolution_convert_fusion.25
  309.1 7.3 fusion.263
  316.7 6.9 convolution_bitcast_fusion
  323.5 6.0 all_to_all.47
  329.6 4.6 copy.91
  334.2 4.8 all-to-all-start.2
  339.1 41.0 %all-reduce.15.cloned.1.call-done = (bf16[128,512]{1,0:T(8,128)(2,1)}, bf16[512,384]{1,0:T(8,128)(2,1)}) async-done(((bf16[128,512]{1,0:T(8,128)(2,1)}, bf16[512,384]{1,0:T(8,128)(2,1)}), (bf16[128,512]{1,0:T(8,128)(2,1)}, bf16[512,384]{1,0:T(8,128)(2,1)})) %all-reduce.15.cloned.1.call-update) | async-done | bytes 524304 | tf_op jit(solution)/shard_map/psum | solution.py:200
  382.1 2.5 maximum_multiply_fusion
  386.2 2.5 maximum_multiply_fusion.1
  388.8 12.2 %all-gather.11.cloned.1.call-done = bf16[512,1536]{1,0:T(8,128)(2,1)} async-done(((bf16[512,384]{1,0:T(8,128)(2,1)}), bf16[512,1536]{1,0:T(8,128)(2,1)}) %all-gather.11.cloned.1.call-update) | async-done | bytes 1572880 | tf_op jit(solution)/shard_map/all_gather | solution.py:190
  401.0 6.1 fusion.269
  407.0 2.9 copy.92
  410.0 3.0 fusion.54
  413.0 131.2 %reduce-scatter.6.cloned.1.call-done = f32[512,64]{0,1:T(8,128)} async-done(((f32[512,2048]{0,1:T(8,128)}), f32[512,64]{0,1:T(8,128)}) %reduce-scatter.6.cloned.1.call-update) | async-done | bytes 131088 | tf_op jit(solution)/shard_map/reduce_scatter | solution.py:165
  545.8 137.6 %reduce-scatter.8.cloned.1.call-done = f32[512,64]{0,1:T(8,128)} async-done(((f32[512,2048]{0,1:T(8,128)}), f32[512,64]{0,1:T(8,128)}) %reduce-scatter.8.cloned.1.call-update) | async-done | bytes 131088 | tf_op jit(solution)/shard_map/reduce_scatter | solution.py:166
  685.0 4.0 maximum_bitcast_fusion
  690.2 11.2 all-reduce.1
  701.4 33.4 %all-reduce = (f32[4,3]{1,0:T(4,128)S(1)}, f32[4,512]{1,0:T(4,128)}) all-reduce(f32[4,3]{1,0:T(4,128)} %get-tuple-element.219, f32[4,512]{1,0:T(4,128)} %get-tuple-element.220), channel_id=1, replica_groups=mesh['dp'=8,'head'=4] {'dp'}, use_global_device_ids=true, to_apply=%region_33.34 | all-reduce | flops 2060 | bytes 16480 | tf_op jit(solution)/shard_map/psum | solution.py:214
  745.0 31.5 %all_gather.27 = bf16[512,512]{0,1:T(8,128)(2,1)S(1)} all-gather(bf16[512,64]{0,1:T(8,128)(2,1)S(1)} %get-tuple-element.243), channel_id=1, replica_groups=mesh['dp'=8,'head'=4] {'dp'}, dimensions={1}, use_global_device_ids=true | all-gather | bytes 589824 | tf_op jit(solution)/shard_map/all_gather | solution.py:228
  779.2 31.2 %all_gather.26 = bf16[512,512]{0,1:T(8,128)(2,1)S(1)} all-gather(bf16[512,64]{0,1:T(8,128)(2,1)S(1)} %get-tuple-element.245), channel_id=1, replica_groups=mesh['dp'=8,'head'=4] {'dp'}, dimensions={1}, use_global_device_ids=true | all-gather | bytes 589824 | tf_op jit(solution)/shard_map/all_gather | solution.py:227
  815.6 48.2 %all-reduce.25.cloned.1.call-done = (bf16[512,512]{1,0:T(8,128)(2,1)}, bf16[512,512]{1,0:T(8,128)(2,1)}, bf16[512,512]{1,0:T(8,128)(2,1)}, bf16[512,512]{1,0:T(8,128)(2,1)}) async-done(((bf16[512,512]{1,0:T(8,128)(2,1)}, bf16[512,512]{1,0:T(8,128)(2,1)}, bf16[512,512]{1,0:T(8,128)(2,1)}, bf16[512,512]{1,0:T(8,128)(2,1)}), (bf16[512,512]{1,0:T(8,128)(2,1)}, bf16[512,512]{1,0:T(8,128)(2,1)}, ...) | async-done | bytes 2097168 | tf_op jit(solution)/shard_map/psum | solution.py:239
  863.8 3.5 fusion.100
  869.7 3.5 fusion.96
  878.9 2.8 fusion.104
  883.0 52.1 %all-reduce.23.cloned.1.call-done = (bf16[512,512]{1,0:T(8,128)(2,1)}, bf16[512,512]{1,0:T(8,128)(2,1)}, bf16[512,512]{1,0:T(8,128)(2,1)}, bf16[512,512]{1,0:T(8,128)(2,1)}) async-done(((bf16[512,512]{1,0:T(8,128)(2,1)}, bf16[512,512]{1,0:T(8,128)(2,1)}, bf16[512,512]{1,0:T(8,128)(2,1)}, bf16[512,512]{1,0:T(8,128)(2,1)}), (bf16[512,512]{1,0:T(8,128)(2,1)}, bf16[512,512]{1,0:T(8,128)(2,1)}, ...) | async-done | bytes 2097168 | tf_op jit(solution)/shard_map/psum | solution.py:239
  935.1 3.5 fusion.101
  941.1 3.5 fusion.97
  947.0 2.8 fusion.130
  951.9 3.0 fusion.105
  957.3 52.1 %all-reduce.21.cloned.1.call-done = (bf16[512,512]{1,0:T(8,128)(2,1)}, bf16[512,512]{1,0:T(8,128)(2,1)}, bf16[512,512]{1,0:T(8,128)(2,1)}, bf16[512,512]{1,0:T(8,128)(2,1)}) async-done(((bf16[512,512]{1,0:T(8,128)(2,1)}, bf16[512,512]{1,0:T(8,128)(2,1)}, bf16[512,512]{1,0:T(8,128)(2,1)}, bf16[512,512]{1,0:T(8,128)(2,1)}), (bf16[512,512]{1,0:T(8,128)(2,1)}, bf16[512,512]{1,0:T(8,128)(2,1)}, ...) | async-done | bytes 2097168 | tf_op jit(solution)/shard_map/psum | solution.py:239
  1009.4 3.4 fusion.102
  1015.3 3.5 fusion.98
  1024.5 2.5 fusion.106
  1028.6 6.8 add_convert_fusion
  1038.3 42.2 %all-reduce.19.cloned.1.call-done = (bf16[512,512]{1,0:T(8,128)(2,1)}, bf16[512,512]{1,0:T(8,128)(2,1)}, bf16[512,512]{1,0:T(8,128)(2,1)}, bf16[512,512]{1,0:T(8,128)(2,1)}) async-done(((bf16[512,512]{1,0:T(8,128)(2,1)}, bf16[512,512]{1,0:T(8,128)(2,1)}, bf16[512,512]{1,0:T(8,128)(2,1)}, bf16[512,512]{1,0:T(8,128)(2,1)}), (bf16[512,512]{1,0:T(8,128)(2,1)}, bf16[512,512]{1,0:T(8,128)(2,1)}, ...) | async-done | bytes 2097168 | tf_op jit(solution)/shard_map/psum | solution.py:239
  1080.5 3.5 fusion.103
  1086.5 3.4 fusion.99
  1095.6 2.6 fusion.107
  1099.5 3.6 fusion.53
  1103.1 2.9 copy.97
  1107.3 44.4 %all-reduce.17.cloned.1.call-done = (bf16[512,512]{1,0:T(8,128)(2,1)}, bf16[512,512]{1,0:T(8,128)(2,1)}, bf16[512,512]{1,0:T(8,128)(2,1)}, bf16[512,512]{1,0:T(8,128)(2,1)}) async-done(((bf16[512,512]{1,0:T(8,128)(2,1)}, bf16[512,512]{1,0:T(8,128)(2,1)}, bf16[512,512]{1,0:T(8,128)(2,1)}, bf16[512,512]{1,0:T(8,128)(2,1)}), (bf16[512,512]{1,0:T(8,128)(2,1)}, bf16[512,512]{1,0:T(8,128)(2,1)}, ...) | async-done | bytes 2097168 | tf_op jit(solution)/shard_map/psum | solution.py:239
  1151.6 3.2 fusion.112
  1160.4 2.8 fusion.127
  (343 shorter events, 224.7 us)
Async XLA Ops:
  7.2 2.1 copy-start.43
  7.2 41.4 %all-gather.5.cloned.1.call-start = ((), (), s32[]{:S(2)}) async-start(), calls=%async_computation.6 | async-start | bytes 5242880 | tf_op jit(solution)/shard_map/all_gather | solution.py:123
  8.9 2.4 copy-start.27
  8.9 3.1 copy-start.25
  9.3 3.5 copy-start.12
  9.9 400.1 %copy-start.36 = (f32[1,512]{1,0:T(1,128)}, f32[1,512]{1,0:T(1,128)S(1)}, u32[]{:S(2)}) copy-start(f32[1,512]{1,0:T(1,128)S(1)} %get-tuple-element.258) | copy-start | bytes 6148
  9.9 3.0 copy-start.40
  11.3 130.4 %all-gather.7.cloned.1.call-start = ((), (), s32[]{:S(2)}) async-start(), calls=%async_computation.7 | async-start | bytes 2162688 | tf_op jit(solution)/shard_map/all_gather | solution.py:141
  12.0 155.1 %all-gather.9.cloned.1.call-start = ((), (), s32[]{:S(2)}) async-start(), calls=%async_computation.8 | async-start | bytes 2162688 | tf_op jit(solution)/shard_map/all_gather | solution.py:142
  12.8 42.0 %copy-start.9 = (bf16[512,384]{1,0:T(8,128)(2,1)}, bf16[512,384]{1,0:T(8,128)(2,1)S(1)}, u32[]{:S(2)}) copy-start(bf16[512,384]{1,0:T(8,128)(2,1)S(1)} %convert_element_type.446) | copy-start | bytes 1179652
  107.7 5.7 copy-start.4
  107.7 5.7 copy-start.33
  113.4 6.2 copy-start.29
  115.9 3.7 copy-start.10
  115.9 22.3 %all-to-all-start = ((bf16[4,1024,128]{1,2,0:T(8,128)(2,1)}), bf16[4,1024,128]{1,2,0:T(8,128)(2,1)S(1)}, u32[]{:S(2)}, u32[]{:S(2)}) async-start(bf16[4,1024,128]{1,2,0:T(8,128)(2,1)} %copy.81), calls=%async_computation | async-start | bytes 2097152 | tf_op jit(solution)/shard_map/all_to_all | solution.py:134
  141.3 41.4 %copy-start = (f32[1024,512]{0,1:T(8,128)}, f32[1024,512]{0,1:T(8,128)S(1)}, u32[]{:S(2)}) copy-start(f32[1024,512]{0,1:T(8,128)S(1)} %get-tuple-element.265) | copy-start | bytes 6291460
  167.2 8.4 copy-start.51
  175.6 4.2 copy-start.53
  182.7 3.0 copy-start.2
  182.7 3.0 copy-start.6
  185.8 2.4 copy-start.5
  189.9 18.8 %all-to-all-start.1 = ((bf16[1024,4,128]{0,2,1:T(8,128)(2,1)}), bf16[1024,4,128]{0,2,1:T(8,128)(2,1)}, u32[]{:S(2)}, u32[]{:S(2)}) async-start(bf16[1024,4,128]{0,2,1:T(8,128)(2,1)} %bitcast.284), calls=%async_computation.1 | async-start | bytes 2097152 | tf_op jit(solution)/shard_map/all_to_all | solution.py:176
  194.1 114.3 %reduce-scatter.4.cloned.1.call-start = ((), (), s32[]{:S(2)}) async-start(), calls=%async_computation.10 | async-start | bytes 655360 | tf_op jit(solution)/shard_map/reduce_scatter | solution.py:180
  197.0 183.1 %all-reduce.15.cloned.1.call-start = ((), (), s32[]{:S(2)}) async-start(), calls=%async_computation.13 | async-start | bytes 1048576 | tf_op jit(solution)/shard_map/psum | solution.py:200
  302.0 2.1 copy-start.1
  302.0 3.3 copy-start.50
  308.5 92.5 %all-gather.11.cloned.1.call-start = ((), (), s32[]{:S(2)}) async-start(), calls=%async_computation.9 | async-start | bytes 1966080 | tf_op jit(solution)/shard_map/all_gather | solution.py:190
  309.0 235.1 %reduce-scatter.6.cloned.1.call-start = ((), (), s32[]{:S(2)}) async-start(), calls=%async_computation.11 | async-start | bytes 4325376 | tf_op jit(solution)/shard_map/reduce_scatter | solution.py:165
  316.4 366.9 %reduce-scatter.8.cloned.1.call-start = ((), (), s32[]{:S(2)}) async-start(), calls=%async_computation.12 | async-start | bytes 4325376 | tf_op jit(solution)/shard_map/reduce_scatter | solution.py:166
  334.1 50.5 %copy-start.11 = (f32[128,512]{1,0:T(8,128)S(1)}, f32[128,512]{1,0:T(8,128)}, u32[]{:S(2)}) copy-start(f32[128,512]{1,0:T(8,128)} %param.27) | copy-start | bytes 786436
  334.2 66.8 %all-to-all-start.2 = ((bf16[4,1024,384]{1,2,0:T(8,128)(2,1)}), bf16[4,1024,384]{1,2,0:T(8,128)(2,1)}, u32[]{:S(2)}, u32[]{:S(2)}) async-start(bf16[4,1024,384]{1,2,0:T(8,128)(2,1)} %copy.91), calls=%async_computation.2 | async-start | bytes 6291456 | tf_op jit(solution)/shard_map/all_to_all | solution.py:189
  339.0 524.8 %all-reduce.25.cloned.1.call-start = ((), (), s32[]{:S(2)}) async-start(), calls=%async_computation.18 | async-start | bytes 4194304 | tf_op jit(solution)/shard_map/psum | solution.py:239
  409.9 3.0 copy-start.41
  409.9 3.0 copy-start.48
  410.0 3.0 copy-start.49
  410.0 330.0 %copy-start.7 = (bf16[512,384]{1,0:T(8,128)(2,1)S(1)}, bf16[512,384]{1,0:T(8,128)(2,1)}, u32[]{:S(2)}) copy-start(bf16[512,384]{1,0:T(8,128)(2,1)} %get-tuple-element.222) | copy-start | bytes 1179652
  742.1 36.4 %copy-start.21 = (f32[512,64]{0,1:T(8,128)S(1)}, f32[512,64]{0,1:T(8,128)}, u32[]{:S(2)}) copy-start(f32[512,64]{0,1:T(8,128)} %param.29) | copy-start | bytes 393220
  742.1 36.4 %copy-start.22 = (f32[512,64]{0,1:T(8,128)S(1)}, f32[512,64]{0,1:T(8,128)}, u32[]{:S(2)}) copy-start(f32[512,64]{0,1:T(8,128)} %reduce-scatter.6.cloned.1.call-done) | copy-start | bytes 393220
  776.5 35.1 %copy-start.23 = (bf16[512,512]{0,1:T(8,128)(2,1)}, bf16[512,512]{0,1:T(8,128)(2,1)S(1)}, u32[]{:S(2)}) copy-start(bf16[512,512]{0,1:T(8,128)(2,1)S(1)} %all_gather.27) | copy-start | bytes 1572868
  776.5 36.4 %copy-start.31 = (f32[128,512]{1,0:T(8,128)S(1)}, f32[128,512]{1,0:T(8,128)}, u32[]{:S(2)}) copy-start(f32[128,512]{1,0:T(8,128)} %fusion.219) | copy-start | bytes 786436
  777.8 36.3 %copy-start.14 = (f32[512,384]{1,0:T(8,128)S(1)}, f32[512,384]{1,0:T(8,128)}, u32[]{:S(2)}) copy-start(f32[512,384]{1,0:T(8,128)} %fusion.174) | copy-start | bytes 2359300
  815.4 119.7 %all-reduce.23.cloned.1.call-start = ((), (), s32[]{:S(2)}) async-start(), calls=%async_computation.17 | async-start | bytes 4194304 | tf_op jit(solution)/shard_map/psum | solution.py:239
  869.7 6.0 copy-start.32
  882.9 126.5 %all-reduce.21.cloned.1.call-start = ((), (), s32[]{:S(2)}) async-start(), calls=%async_computation.16 | async-start | bytes 4194304 | tf_op jit(solution)/shard_map/psum | solution.py:239
  957.3 123.2 %all-reduce.19.cloned.1.call-start = ((), (), s32[]{:S(2)}) async-start(), calls=%async_computation.15 | async-start | bytes 4194304 | tf_op jit(solution)/shard_map/psum | solution.py:239
  1015.3 6.0 copy-start.20
  1027.0 8.4 copy-start.8
  1028.3 123.3 %all-reduce.17.cloned.1.call-start = ((), (), s32[]{:S(2)}) async-start(), calls=%async_computation.14 | async-start | bytes 4194304 | tf_op jit(solution)/shard_map/psum | solution.py:239
  1035.4 2.3 copy-start.39
  1086.5 5.9 copy-start.18
  1098.2 1.3 copy-start.38
  1098.2 1.3 copy-start.37
  1103.1 3.0 copy-start.35
  1103.1 3.0 copy-start.46
  1103.1 3.6 copy-start.42
  1103.1 48.6 %copy-start.44 = (bf16[512,512]{0,1:T(8,128)(2,1)S(1)}, bf16[512,512]{0,1:T(8,128)(2,1)}, u32[]{:S(2)}) copy-start(bf16[512,512]{0,1:T(8,128)(2,1)} %fusion.103) | copy-start | bytes 1572868
  1106.0 48.8 %copy-start.45 = (bf16[512,512]{0,1:T(8,128)(2,1)S(1)}, bf16[512,512]{0,1:T(8,128)(2,1)}, u32[]{:S(2)}) copy-start(bf16[512,512]{0,1:T(8,128)(2,1)} %fusion.99) | copy-start | bytes 1572868
  1106.7 50.5 %copy-start.34 = (f32[4,512]{1,0:T(4,128)}, f32[4,512]{1,0:T(4,128)S(1)}, u32[]{:S(2)}) copy-start(f32[4,512]{1,0:T(4,128)S(1)} %get-tuple-element.248) | copy-start | bytes 24580
  1154.9 2.3 copy-start.26
  1154.9 4.0 copy-start.28
  1154.9 5.6 copy-start.16
  1154.9 5.6 copy-start.30
  1157.2 6.1 copy-start.13
  1158.9 4.4 copy-start.52
  (6 other events, 6.4 us)
Sparse Core Ops, SparseCore 0:
  11.4 37.1 all-gather.4
  52.0 56.3 all-gather.6
  111.9 55.2 all-gather.8
  197.7 21.9 reduce-scatter.3
  308.6 71.4 all-reduce.14
  382.1 18.8 all-gather.10
  403.2 140.9 reduce-scatter.5
  546.5 136.8 reduce-scatter.7
  815.5 48.2 all-reduce.24
  883.1 51.9 all-reduce.22
  957.4 52.0 all-reduce.20
  1028.4 51.9 all-reduce.18
  1099.6 52.0 all-reduce.16
